TPU v7x, 256 devices: a whole 4x4x8 slice. The times are simulated.
256 devices in a mesh: pole: 4 (over y), row: 8 (over z_lo, x), col: 8 (over z_hi, core).
Axes of the slice: x: 4, y: 4, z: 8 (z_hi: 4, z_lo: 2; z = z_hi * 2 + z_lo), core: 2. Of those that a mesh axis runs over, the one named last changes fastest.
Arguments:
- found_inverse: bfloat16 [4, 2, 8192, 8, 8, 128], P('pole', None, 'row', None, 'col'), may hold values from -0.125 to 0.125
- l_panel: bfloat16 [4, 2, 8192, 512], P('pole', None, ('row', 'col')), may hold values from -1.5 to 1.5
- block_pattern: int32 [64, 4], P(('row', 'col')), may hold values 0 or 1
- sup_widths: int32 [4], replicated, may hold values from 1 to 128, 320 in all
- diag_inverse: bfloat16 [4, 2, 512, 128], P('pole'), may hold values from -6 to 6
- pole_weights: float32 [4, 2], P('pole'), may hold values from -4 to 4
Outputs:
- density: float32 [512, 8192], P('col', 'row')
- diagonal: float32 [512, 128], replicated
Inputs may be any that keep to these rules, and one draw needn't show every extreme that they name: `sup_widths`: one supernode has exactly 128 columns.
All inputs are finite; a program needn't handle non-finite values. No bound on the sum of `block_pattern` on one device may be relied on, other than what follows from the above.
Results may differ from a plain program's by a relative error of at most 0.0003.
Values may be sent and summed in bfloat16 or wider, within the bound.
A program may use at most 128 MiB of HBM per device.

v0:
```python
import jax
import jax.numpy as jnp
from jax import lax
from jax.sharding import PartitionSpec as P


def contract(left, right):
    return jnp.einsum("jk,ij->ki", left, right, preferred_element_type=jnp.float32)


def pair_product(left, right):
    return jnp.einsum("ika,kbi->kab", left, right, precision=lax.Precision.HIGHEST)


def per_device(found_inverse, l_panel, block_pattern, sup_widths, diag_inverse, pole_weights):
    slot_width = diag_inverse.shape[-1]
    total_cols = l_panel.shape[-1]
    supernodes = total_cols // slot_width
    row_count = lax.axis_size("row")
    row_index = lax.axis_index("row")
    col_index = lax.axis_index("col")
    columns = jnp.arange(total_cols, dtype=jnp.int32)
    column_ok = columns % slot_width < jnp.repeat(sup_widths, slot_width)
    block_ok = jnp.repeat(block_pattern[0], slot_width) == 1
    masked = jnp.where(
        (column_ok & block_ok)[None, None, :], l_panel[0], jnp.zeros((), jnp.bfloat16)
    )
    column_rows = lax.all_gather(masked, "row", axis=1, tiled=True)
    own_rows = lax.all_gather(masked, "col", axis=1, tiled=True)
    local_rows = found_inverse.shape[2]
    inverse = found_inverse[0].reshape(2, local_rows, row_count * slot_width)
    part_real = contract(column_rows[1], inverse[1]) - contract(column_rows[0], inverse[0])
    part_imag = -(contract(column_rows[1], inverse[0]) + contract(column_rows[0], inverse[1]))
    w_real = pole_weights[0, 0]
    w_imag = pole_weights[0, 1]
    weighted = w_real * part_real - w_imag * part_imag
    part = lax.psum_scatter(weighted, "col", scatter_dimension=0, tiled=True)
    density = lax.psum(part, "pole")
    lifted = own_rows.astype(jnp.float32).reshape(2, local_rows, supernodes, slot_width)
    upper_real = part_real.reshape(supernodes, slot_width, local_rows)
    upper_imag = part_imag.reshape(supernodes, slot_width, local_rows)
    t_real = pair_product(lifted[0], upper_real) - pair_product(lifted[1], upper_imag)
    t_imag = pair_product(lifted[0], upper_imag) + pair_product(lifted[1], upper_real)
    lead_flag = ((row_index == 0) & (col_index == 0)).astype(jnp.float32)
    d_real = diag_inverse[0, 0].astype(jnp.float32).reshape(supernodes, slot_width, slot_width)
    d_imag = diag_inverse[0, 1].astype(jnp.float32).reshape(supernodes, slot_width, slot_width)
    local_term = lead_flag * (w_real * d_real - w_imag * d_imag) - (
        w_real * t_real - w_imag * t_imag
    )
    diagonal = lax.psum(local_term.reshape(total_cols, slot_width), ("pole", "row", "col"))
    return (density, diagonal)


def solution(mesh):
    in_specs = (
        P("pole", None, "row", None, "col", None),
        P("pole", None, ("row", "col"), None),
        P(("row", "col"), None),
        P(),
        P("pole", None, None, None),
        P("pole", None),
    )
    out_specs = (P("col", "row"), P())
    return jax.shard_map(
        per_device, mesh=mesh, in_specs=in_specs, out_specs=out_specs, check_vma=False
    )
```

profile of v0, /device:TPU:2, one launch (start us, length us, event | category | flops | bytes accessed | tf_op | source)
XLA Modules:
  0.0 457.6 jit_solution(11535285280863356408)
XLA Ops:
  7.2 0.0 all-gather.3.cloned.1.call-start
  7.2 0.7 compare_bitcast_fusion
  7.9 0.7 fusion.25
  8.6 1.7 bitcast_select_fusion
  10.3 0.0 all-gather.3.cloned.1.call-update
  10.3 0.0 all-gather.5.cloned.1.call-start
  10.3 0.7 all-gather.5.cloned.1.call-update
  11.1 0.0 reduce-scatter.2.cloned.1.call-start
  11.1 1.4 fusion.28
  12.5 3.8 fusion.26
  16.3 38.6 %all-gather.3.cloned.1.call-done = bf16[2,1024,512]{2,1,0:T(8,128)(2,1)} async-done(((bf16[2,128,512]{2,1,0:T(8,128)(2,1)}), bf16[2,1024,512]{2,1,0:T(8,128)(2,1)}) %all-gather.3.cloned.1.call-update) | async-done | bytes 2097168 | tf_op jit(solution)/shard_map/all_gather | solution.py:28
  54.9 0.0 copy-start.3
  54.9 2.7 fusion.2
  57.6 0.0 copy-done.3
  57.6 0.0 copy-start.2
  57.6 1.3 fusion
  58.9 0.3 copy-done.2
  59.2 1.3 fusion.12
  60.5 4.6 %multiply_subtract_fusion = (f32[512,1024]{1,0:T(8,128)}, f32[512,1024]{1,0:T(8,128)}) fusion(f32[512,1024]{1,0:T(8,128)S(1)} %fusion.12, f32[]{:T(128)} %bitcast.7, f32[]{:T(128)} %bitcast, f32[512,1024]{1,0:T(8,128)S(1)} %fusion, bf16[128,8,8,128]{3,2,1,0:T(8,128)(2,1)S(1)} %bitcast.67, bf16[2,1024,512]{2,1,0:T(8,128)(2,1)S(1)} %copy-done.3), kind=kOutput, calls=%fused_computation.8 | convolution fusion | flops 1076363264 | bytes 11534344 | tf_op jit(solution)/shard_map/jk,ij->ki/dot_general | solution.py:8
  65.1 0.0 copy-start.4
  65.1 0.0 reduce-scatter.2.cloned.1.call-update
  65.1 0.0 all-reduce.5.cloned.1.call-start
  65.2 0.9 copy-done.4
  66.1 1.3 subtract_multiply_fusion
  67.4 27.9 %all-gather.5.cloned.1.call-done = bf16[2,1024,512]{2,1,0:T(8,128)(2,1)} async-done(((bf16[2,128,512]{2,1,0:T(8,128)(2,1)}), bf16[2,1024,512]{2,1,0:T(8,128)(2,1)}) %all-gather.5.cloned.1.call-update) | async-done | bytes 2097168 | tf_op jit(solution)/shard_map/all_gather | solution.py:29
  95.3 2.7 fusion.27
  97.9 1.3 copy.8
  99.3 1.5 copy.9
  100.8 0.0 copy-start
  100.8 0.0 copy-start.1
  100.8 2.5 fusion.29
  103.3 0.0 copy-done
  103.3 0.0 copy-done.1
  103.3 1.2 fusion.30
  104.5 1.9 fusion.20
  106.4 2.5 fusion.19
  108.9 0.0 all-reduce.5.cloned.1.call-update
  108.9 0.0 all-reduce.3.cloned.1.call-start
  109.0 31.0 %reduce-scatter.2.cloned.1.call-done = f32[64,1024]{1,0:T(8,128)} async-done(((f32[512,1024]{1,0:T(8,128)}), f32[64,1024]{1,0:T(8,128)}) %reduce-scatter.2.cloned.1.call-update) | async-done | bytes 262160 | tf_op jit(solution)/shard_map/reduce_scatter | solution.py:37
  140.0 0.0 all-reduce.3.cloned.1.call-update
  140.1 259.7 %all-reduce.5.cloned.1.call-done = f32[512,128]{1,0:T(8,128)} async-done(((f32[512,128]{1,0:T(8,128)}), f32[512,128]{1,0:T(8,128)}) %all-reduce.5.cloned.1.call-update) | async-done | bytes 262160 | tf_op jit(solution)/shard_map/psum | solution.py:50
  399.8 48.0 %all-reduce.3.cloned.1.call-done = f32[64,1024]{1,0:T(8,128)} async-done(((f32[64,1024]{1,0:T(8,128)}), f32[64,1024]{1,0:T(8,128)}) %all-reduce.3.cloned.1.call-update) | async-done | bytes 262160 | tf_op jit(solution)/shard_map/psum | solution.py:38
  447.8 1.7 copy.36
  449.4 1.7 copy.37
Async XLA Ops:
  7.2 47.7 %all-gather.3.cloned.1.call-start = ((), (), s32[]{:S(2)}) async-start(), calls=%async_computation.1 | async-start | bytes 2359296 | tf_op jit(solution)/shard_map/all_gather | solution.py:28
  10.3 85.0 %all-gather.5.cloned.1.call-start = ((), (), s32[]{:S(2)}) async-start(), calls=%async_computation.4 | async-start | bytes 2359296 | tf_op jit(solution)/shard_map/all_gather | solution.py:29
  11.1 129.0 %reduce-scatter.2.cloned.1.call-start = ((), (), s32[]{:S(2)}) async-start(), calls=%async_computation.2 | async-start | bytes 2359296 | tf_op jit(solution)/shard_map/reduce_scatter | solution.py:37
  54.9 2.7 copy-start.3
  57.6 1.6 copy-start.2
  65.1 0.9 copy-start.4
  65.1 334.7 %all-reduce.5.cloned.1.call-start = ((), (), s32[]{:S(2)}) async-start(), calls=%async_computation.5 | async-start | bytes 524288 | tf_op jit(solution)/shard_map/psum | solution.py:50
  100.8 2.6 copy-start
  100.8 2.6 copy-start.1
  108.9 338.8 %all-reduce.3.cloned.1.call-start = ((), (), s32[]{:S(2)}) async-start(), calls=%async_computation.3 | async-start | bytes 524288 | tf_op jit(solution)/shard_map/psum | solution.py:38
Sparse Core Ops, SparseCore 0:
  10.4 44.4 all-gather.2
  57.3 37.9 all-gather.4
  97.8 42.1 reduce-scatter.1
  145.9 253.8 all-reduce.4
  402.0 45.7 all-reduce.2
where the time goes:
time: 458 us
  waiting for transfers between devices  406 us (89%)
  matrix products  18 us (4%)
  local copies, waits for them, and re-layouts  15.2 us (3%)
  between operations  13.9 us (3%)
    psum x1, waiting for transfers between devices, per_device(): lax.psum(local_term.reshape(total_cols, slot_width), ('pole', 'row', 'col'))  260 us
    psum x1, waiting for transfers between devices, per_device(): density = lax.psum(part, 'pole')  48 us
    all_gather x1, waiting for transfers between devices, per_device(): column_rows = lax.all_gather(masked, 'row', axis=1, tiled=True)  38.6 us
    reduce_scatter x1, waiting for transfers between devices, per_device(): part = lax.psum_scatter(weighted, 'col', scatter_dimension=0, tiled=True)  31 us
    all_gather x1, waiting for transfers between devices, per_device(): own_rows = lax.all_gather(masked, 'col', axis=1, tiled=True)  27.9 us
    dot_general x4, matrix products, contract(): jnp.einsum('jk,ij->ki', left, right, preferred_element_type=jnp.float32)  9.92 us
  transfers between devices with their start and end apart: 5, of which 5 were waited for; matrix products, arithmetic and copies ran while one was open for 7% of the time, Pallas kernels for 0%

commit v1 on v0

--- a/solution.py
+++ b/solution.py
@@ -47,7 +47,8 @@
     local_term = lead_flag * (w_real * d_real - w_imag * d_imag) - (
         w_real * t_real - w_imag * t_imag
     )
-    diagonal = lax.psum(local_term.reshape(total_cols, slot_width), ("pole", "row", "col"))
+    one_axis = lax.psum(local_term.reshape(total_cols, slot_width), "pole")
+    diagonal = lax.psum(one_axis, ("row", "col"))
     return (density, diagonal)
 
 

time: 458 us -> 384 us (0.84)
  waiting for transfers between devices: 406 us -> 330 us
    psum x1, waiting for transfers between devices: 260 us -> 180 us  [per_device(): diagonal = lax.psum(one_axis, ('row', 'col'))]
  transfers between devices with their start and end apart: 5 -> 5, of which waited for: 5 -> 5; matrix products, arithmetic and copies ran while one was open for 7% -> 8% of each run, Pallas kernels for 0% -> 0%
where the time goes in v1:
time: 384 us; the launch traced here: 381 us
  waiting for transfers between devices  330 us (86%)
  matrix products  17.9 us (5%)
  local copies, waits for them, and re-layouts  15.1 us (4%)
  between operations  13.9 us (4%)
  other arithmetic  4.31 us (1%)
    psum x1, waiting for transfers between devices, per_device(): diagonal = lax.psum(one_axis, ('row', 'col'))  180 us
    psum x1, waiting for transfers between devices, per_device(): density = lax.psum(part, 'pole')  50.8 us
    all_gather x1, waiting for transfers between devices, per_device(): column_rows = lax.all_gather(masked, 'row', axis=1, tiled=True)  38.6 us
    reduce_scatter x1, waiting for transfers between devices, per_device(): part = lax.psum_scatter(weighted, 'col', scatter_dimension=0, tiled=True)  31.2 us
    all_gather x1, waiting for transfers between devices, per_device(): own_rows = lax.all_gather(masked, 'col', axis=1, tiled=True)  27.9 us
    dot_general x4, matrix products, contract(): jnp.einsum('jk,ij->ki', left, right, preferred_element_type=jnp.float32)  9.92 us
    dot_general x4, matrix products, pair_product(): jnp.einsum('ika,kbi->kab', left, right, precision=lax.Precision.HIGHEST)  8.03 us
  transfers between devices with their start and end apart: 5, of which 5 were waited for; matrix products, arithmetic and copies ran while one was open for 8% of the time, Pallas kernels for 0%

profile of v1, /device:TPU:2, one launch (start us, length us, event | category | flops | bytes accessed | tf_op | source)
XLA Modules:
  0.0 381.0 jit_solution(16032095371703476693)
XLA Ops:
  7.2 0.0 all-gather.3.cloned.1.call-start
  7.2 0.7 compare_bitcast_fusion
  7.9 0.7 fusion.25
  8.6 1.7 bitcast_select_fusion
  10.3 0.0 all-gather.3.cloned.1.call-update
  10.3 0.0 all-gather.5.cloned.1.call-start
  10.3 0.7 all-gather.5.cloned.1.call-update
  11.1 0.0 reduce-scatter.2.cloned.1.call-start
  11.1 1.3 fusion.28
  12.4 3.8 %fusion.26 = (bf16[1,1,1024,8,1,128]{5,3,4,2,1,0:T(8,128)(2,1)}, bf16[1,1,1024,8,1,128]{5,3,4,2,1,0:T(8,128)(2,1)S(1)}) fusion(bf16[1,2,1024,8,1,128]{5,3,4,2,1,0:T(8,128)(2,1)} %param.6), kind=kLoop, calls=%fused_computation.33 | loop fusion | bytes 8388608 | tf_op jit(solution)/shard_map/slice | solution.py:32
  16.2 38.6 %all-gather.3.cloned.1.call-done = bf16[2,1024,512]{2,1,0:T(8,128)(2,1)} async-done(((bf16[2,128,512]{2,1,0:T(8,128)(2,1)}), bf16[2,1024,512]{2,1,0:T(8,128)(2,1)}) %all-gather.3.cloned.1.call-update) | async-done | bytes 2097168 | tf_op jit(solution)/shard_map/all_gather | solution.py:28
  54.9 0.0 copy-start.3
  54.9 2.7 fusion.2
  57.6 0.0 copy-done.3
  57.6 0.0 copy-start.2
  57.6 1.3 fusion
  58.9 0.3 copy-done.2
  59.2 1.3 fusion.12
  60.5 4.6 %multiply_subtract_fusion = (f32[512,1024]{1,0:T(8,128)}, f32[512,1024]{1,0:T(8,128)}) fusion(f32[512,1024]{1,0:T(8,128)S(1)} %fusion.12, f32[]{:T(128)} %bitcast.7, f32[]{:T(128)} %bitcast, f32[512,1024]{1,0:T(8,128)S(1)} %fusion, bf16[128,8,8,128]{3,2,1,0:T(8,128)(2,1)S(1)} %bitcast.67, bf16[2,1024,512]{2,1,0:T(8,128)(2,1)S(1)} %copy-done.3), kind=kOutput, calls=%fused_computation.8 | convolution fusion | flops 1076363264 | bytes 11534344 | tf_op jit(solution)/shard_map/jk,ij->ki/dot_general | solution.py:8
  65.1 0.0 copy-start.4
  65.1 0.0 reduce-scatter.2.cloned.1.call-update
  65.1 0.0 all-reduce.6.cloned.1.call-start
  65.2 0.9 copy-done.4
  66.1 1.2 subtract_multiply_fusion
  67.3 27.9 %all-gather.5.cloned.1.call-done = bf16[2,1024,512]{2,1,0:T(8,128)(2,1)} async-done(((bf16[2,128,512]{2,1,0:T(8,128)(2,1)}), bf16[2,1024,512]{2,1,0:T(8,128)(2,1)}) %all-gather.5.cloned.1.call-update) | async-done | bytes 2097168 | tf_op jit(solution)/shard_map/all_gather | solution.py:29
  95.2 2.7 fusion.27
  97.9 1.3 copy.8
  99.2 1.5 copy.9
  100.7 0.0 copy-start
  100.7 0.0 copy-start.1
  100.7 2.5 fusion.29
  103.3 0.0 copy-done
  103.3 0.0 copy-done.1
  103.3 1.2 fusion.30
  104.5 1.9 fusion.20
  106.4 2.4 fusion.19
  108.8 31.2 %reduce-scatter.2.cloned.1.call-done = f32[64,1024]{1,0:T(8,128)} async-done(((f32[512,1024]{1,0:T(8,128)}), f32[64,1024]{1,0:T(8,128)}) %reduce-scatter.2.cloned.1.call-update) | async-done | bytes 262160 | tf_op jit(solution)/shard_map/reduce_scatter | solution.py:37
  140.0 0.0 all-reduce.6.cloned.1.call-update
  140.0 0.0 all-reduce.4.cloned.1.call-start
  140.0 50.8 %all-reduce.6.cloned.1.call-done = (f32[64,1024]{1,0:T(8,128)}, f32[512,128]{1,0:T(8,128)}) async-done(((f32[64,1024]{1,0:T(8,128)}, f32[512,128]{1,0:T(8,128)}), (f32[64,1024]{1,0:T(8,128)}, f32[512,128]{1,0:T(8,128)})) %all-reduce.6.cloned.1.call-update) | async-done | bytes 524304 | tf_op jit(solution)/shard_map/psum | solution.py:38
  190.9 0.0 all-reduce.4.cloned.1.call-update
  190.9 180.2 %all-reduce.4.cloned.1.call-done = f32[512,128]{1,0:T(8,128)} async-done(((f32[512,128]{1,0:T(8,128)}), f32[512,128]{1,0:T(8,128)}) %all-reduce.4.cloned.1.call-update) | async-done | bytes 262160 | tf_op jit(solution)/shard_map/psum | solution.py:51
  371.1 1.7 copy.37
  372.8 1.7 copy.38
Async XLA Ops:
  7.2 47.7 %all-gather.3.cloned.1.call-start = ((), (), s32[]{:S(2)}) async-start(), calls=%async_computation.1 | async-start | bytes 2359296 | tf_op jit(solution)/shard_map/all_gather | solution.py:28
  10.3 84.9 %all-gather.5.cloned.1.call-start = ((), (), s32[]{:S(2)}) async-start(), calls=%async_computation.3 | async-start | bytes 2359296 | tf_op jit(solution)/shard_map/all_gather | solution.py:29
  11.1 128.9 %reduce-scatter.2.cloned.1.call-start = ((), (), s32[]{:S(2)}) async-start(), calls=%async_computation.2 | async-start | bytes 2359296 | tf_op jit(solution)/shard_map/reduce_scatter | solution.py:37
  54.9 2.7 copy-start.3
  57.6 1.6 copy-start.2
  65.1 0.9 copy-start.4
  65.1 125.8 %all-reduce.6.cloned.1.call-start = ((), (), s32[]{:S(2)}) async-start(), calls=%async_computation.5 | async-start | bytes 1048576 | tf_op jit(solution)/shard_map/psum | solution.py:38
  100.7 2.6 copy-start
  100.7 2.6 copy-start.1
  140.0 231.1 %all-reduce.4.cloned.1.call-start = ((), (), s32[]{:S(2)}) async-start(), calls=%async_computation.4 | async-start | bytes 524288 | tf_op jit(solution)/shard_map/psum | solution.py:51
Sparse Core Ops, SparseCore 0:
  10.4 44.4 all-gather.2
  57.3 37.9 all-gather.4
  97.8 42.1 reduce-scatter.1
  142.8 48.0 all-reduce.5
  194.2 176.8 all-reduce.3
